TPU v7x, 512 devices: a whole 4x8x8 slice. The times are simulated.
512 devices in a mesh: dp: 32 (over x, z), tensor: 16 (over y, core).
Axes of the slice: x: 4, y: 8, z: 8, core: 2. Of those that a mesh axis runs over, the one named last changes fastest.
Arguments:
- tokens: bfloat16 [8192, 4096], P('dp', 'tensor'), may hold values from -6 to 6
- out_grad: bfloat16 [8192, 4096], P('dp', 'tensor'), may hold values from -0.59765625 to 0.59765625
- w_in: bfloat16 [384, 128, 128], P('tensor'), may hold values from -0.25 to 0.25
- w_out: bfloat16 [384, 128, 128], P('tensor'), may hold values from -0.25 to 0.25
- block_rows: int32 [16, 24], P('tensor'), may hold values from -1 to 31, as said below
- block_cols: int32 [16, 24], P('tensor'), may hold values from -1 to 6, as said below
Outputs:
- in_grad: bfloat16 [8192, 4096], P('dp')
- win_grad: float32 [384, 16384], P('tensor', 'dp')
- wout_grad: float32 [384, 16384], P('tensor', 'dp')
Inputs may be any that keep to these rules, and one draw needn't show every extreme that they name: `block_rows`: -1 marks an empty slot; the live slots of one tensor index name distinct blocks; at least 12 slots of each tensor index are live, and all 24 slots of some tensor index are live. `block_cols`: -1 exactly where block_rows is -1.
All inputs are finite; a program needn't handle non-finite values.
Results may differ from a plain program's by a relative error of at most 0.02.
Values may be sent and summed in bfloat16 or wider, within the bound.
No kernel may reach another device: no remote copies, remote signals or barrier semaphores. Data moves between devices by JAX's collectives and lax.ppermute only.
A program may use at most 64 MiB of HBM per device.

v0:
```python
import jax
import jax.numpy as jnp
from jax import lax
from jax.sharding import PartitionSpec as P

FF = 14336
highest = lax.Precision.HIGHEST
clip_limit = 4.0


def local(tokens, out_grad, w_in, w_out, block_rows, block_cols):
    bin_scale = 4194304.0 / lax.axis_size("dp")
    whole_tokens, whole_grad = (
        lax.all_gather(tokens, "tensor", axis=1, tiled=True),
        lax.all_gather(out_grad, "tensor", axis=1, tiled=True),
    )
    tok_count = whole_tokens.shape[0]
    width = whole_tokens.shape[1]
    side = w_in.shape[1]
    row_count = width // side
    col_count = FF // side // lax.axis_size("tensor")
    rows = block_rows[0]
    cols = block_cols[0]
    live = rows >= 0
    livef = live.astype(jnp.float32)
    safe_rows = jnp.where(live, rows, 0)
    safe_cols = jnp.where(live, cols, 0)
    col_hot = (safe_cols[:, None] == jnp.arange(col_count, dtype=jnp.int32)[None, :]).astype(
        jnp.float32
    ) * livef[:, None]
    row_hot = (safe_rows[:, None] == jnp.arange(row_count, dtype=jnp.int32)[None, :]).astype(
        jnp.float32
    ) * livef[:, None]
    in_blocks = whole_tokens.reshape(tok_count, row_count, side).transpose(1, 0, 2)
    grad_blocks = whole_grad.reshape(tok_count, row_count, side).transpose(1, 0, 2)
    picked = jnp.take(in_blocks, safe_rows, axis=0)
    picked_grad = jnp.take(grad_blocks, safe_rows, axis=0)
    slot_pre = jnp.einsum("stk,skh->sth", picked, w_in, preferred_element_type=jnp.float32)
    pre = jnp.einsum("sc,sth->cth", col_hot, slot_pre, precision=highest)
    hidden = jax.nn.silu(pre).astype(jnp.bfloat16)
    slot_back = jnp.einsum("std,shd->sth", picked_grad, w_out, preferred_element_type=jnp.float32)
    dhidden = jnp.einsum("sc,sth->cth", col_hot, slot_back, precision=highest)
    sigma = jax.nn.sigmoid(pre)
    dpre = (dhidden * sigma * (1.0 + pre * (1.0 - sigma))).astype(jnp.bfloat16)
    dpre_picked = jnp.take(dpre, safe_cols, axis=0)
    hidden_picked = jnp.take(hidden, safe_cols, axis=0)
    slot_terms = jnp.einsum("sth,sdh->std", dpre_picked, w_in, preferred_element_type=jnp.float32)
    partial_grad = jnp.einsum("sr,std->rtd", row_hot, slot_terms, precision=highest)
    summed = lax.psum(partial_grad.astype(jnp.bfloat16), "tensor")
    in_grad = summed.transpose(1, 0, 2).reshape(tok_count, width)
    grad_in = (
        jnp.einsum("stk,sth->skh", picked, dpre_picked, preferred_element_type=jnp.float32)
        * livef[:, None, None]
    )
    grad_out = (
        jnp.einsum("sth,std->shd", hidden_picked, picked_grad, preferred_element_type=jnp.float32)
        * livef[:, None, None]
    )
    slot_count = grad_in.shape[0]
    bins_in = jnp.floor(jnp.clip(grad_in, -clip_limit, clip_limit) * bin_scale).reshape(
        slot_count, side * side
    )
    bins_out = jnp.floor(jnp.clip(grad_out, -clip_limit, clip_limit) * bin_scale).reshape(
        slot_count, side * side
    )
    total_in, total_out = (
        lax.psum_scatter(
            bins_in.astype(jnp.bfloat16), "dp", scatter_dimension=1, tiled=True
        ).astype(jnp.float32),
        lax.psum_scatter(
            bins_out.astype(jnp.bfloat16), "dp", scatter_dimension=1, tiled=True
        ).astype(jnp.float32),
    )
    win_grad = total_in / bin_scale
    wout_grad = total_out / bin_scale
    return (in_grad, win_grad, wout_grad)


def solution(mesh):
    in_specs = (
        P("dp", "tensor"),
        P("dp", "tensor"),
        P("tensor", None, None),
        P("tensor", None, None),
        P("tensor", None),
        P("tensor", None),
    )
    out_specs = (P("dp", None), P("tensor", "dp"), P("tensor", "dp"))
    return jax.shard_map(local, mesh=mesh, in_specs=in_specs, out_specs=out_specs, check_vma=False)
```

profile of v0, /device:TPU:1, one launch (start us, length us, event | category | flops | bytes accessed | tf_op | source)
XLA Modules:
  0.0 698.1 jit_solution(12155008888850396349)
XLA Ops:
  7.2 1.7 copy.18
  9.0 1.7 copy.15
  10.7 0.0 reduce-scatter.3.cloned.1.call-start
  10.8 0.7 compare_and_fusion
  11.5 46.5 %all-gather.5.cloned.1.call-done = bf16[256,4096]{0,1:T(8,128)(2,1)} async-done(((bf16[256,256]{0,1:T(8,128)(2,1)}), bf16[256,4096]{0,1:T(8,128)(2,1)}) %all-gather.5.cloned.1.call-update) | async-done | bytes 2097168 | tf_op jit(solution)/shard_map/all_gather | solution.py:14
  58.0 3.2 copy.19
  61.2 40.3 %all-gather.3.cloned.1.call-done = bf16[256,4096]{0,1:T(8,128)(2,1)} async-done(((bf16[256,256]{0,1:T(8,128)(2,1)}), bf16[256,4096]{0,1:T(8,128)(2,1)}) %all-gather.3.cloned.1.call-update) | async-done | bytes 2097168 | tf_op jit(solution)/shard_map/all_gather | solution.py:15
  101.5 4.1 copy.16
  105.6 1.9 gather_fusion.1
  107.5 2.4 gather_fusion
  110.0 2.6 fusion.25
  112.6 3.6 multiply_convert_fusion
  116.2 0.6 fusion.24
  116.8 3.7 fusion.20
  120.6 0.1 copy.21
  120.6 0.8 gather_fusion.2
  121.5 2.3 floor_convert_fusion.1
  123.8 1.4 copy.52
  125.3 0.2 reduce-scatter.5.cloned.1.call-start
  125.5 0.1 copy.24
  125.6 1.9 gather_fusion.3
  127.5 2.8 floor_convert_fusion
  130.3 1.4 copy.51
  131.8 0.6 fusion.26
  132.5 6.7 fusion.6
  139.2 2.3 copy.50
  141.5 198.4 %reduce-scatter.3.cloned.1.call-done = bf16[24,512]{1,0:T(8,128)(2,1)} async-done(((bf16[24,16384]{1,0:T(8,128)(2,1)}), bf16[24,512]{1,0:T(8,128)(2,1)}) %reduce-scatter.3.cloned.1.call-update) | async-done | bytes 24592 | tf_op jit(solution)/shard_map/reduce_scatter | solution.py:67
  339.9 1.4 convert_multiply_fusion.1
  341.2 221.7 %reduce-scatter.5.cloned.1.call-done = bf16[24,512]{1,0:T(8,128)(2,1)} async-done(((bf16[24,16384]{1,0:T(8,128)(2,1)}), bf16[24,512]{1,0:T(8,128)(2,1)}) %reduce-scatter.5.cloned.1.call-update) | async-done | bytes 24592 | tf_op jit(solution)/shard_map/reduce_scatter | solution.py:70
  562.9 1.4 convert_multiply_fusion
  564.3 124.2 %all-reduce.2.cloned.1.call-done = bf16[256,4096]{1,0:T(8,128)(2,1)} async-done(((bf16[256,4096]{1,0:T(8,128)(2,1)}), bf16[256,4096]{1,0:T(8,128)(2,1)}) %all-reduce.2.cloned.1.call-update) | async-done | bytes 2097168 | tf_op jit(solution)/shard_map/psum | solution.py:49
  688.4 3.1 copy.54
  (20 shorter events, 0.2 us)
Async XLA Ops:
  7.2 102.8 %copy-start = (bf16[24,128,128]{2,1,0:T(8,128)(2,1)S(1)}, bf16[24,128,128]{2,1,0:T(8,128)(2,1)}, u32[]{:S(2)}) copy-start(bf16[24,128,128]{2,1,0:T(8,128)(2,1)} %param.12) | copy-start | bytes 2359300
  7.2 50.8 %all-gather.5.cloned.1.call-start = ((), (), s32[]{:S(2)}) async-start(), calls=%async_computation.3 | async-start | bytes 2228224 | tf_op jit(solution)/shard_map/all_gather | solution.py:14
  9.0 92.5 %all-gather.3.cloned.1.call-start = ((), (), s32[]{:S(2)}) async-start(), calls=%async_computation.2 | async-start | bytes 2228224 | tf_op jit(solution)/shard_map/all_gather | solution.py:15
  10.7 329.2 %reduce-scatter.3.cloned.1.call-start = ((), (), s32[]{:S(2)}) async-start(), calls=%async_computation.5 | async-start | bytes 811008 | tf_op jit(solution)/shard_map/reduce_scatter | solution.py:67
  110.0 6.2 copy-start.1
  112.6 3.6 copy-start.2
  125.3 437.6 %reduce-scatter.5.cloned.1.call-start = ((), (), s32[]{:S(2)}) async-start(), calls=%async_computation.6 | async-start | bytes 811008 | tf_op jit(solution)/shard_map/reduce_scatter | solution.py:70
  130.3 1.5 copy-start.3
  131.8 556.7 %all-reduce.2.cloned.1.call-start = ((), (), s32[]{:S(2)}) async-start(), calls=%async_computation.4 | async-start | bytes 4194304 | tf_op jit(solution)/shard_map/psum | solution.py:49
Sparse Core Ops, SparseCore 0:
  10.1 47.7 all-gather.4
  60.7 40.7 all-gather.2
  125.4 214.4 reduce-scatter.2
  344.1 218.7 reduce-scatter.4
  565.7 122.7 all-reduce.1
where the time goes:
time: 699 us; the launch traced here: 698 us
  waiting for transfers between devices  631 us (90%)
  local copies, waits for them, and re-layouts  26.2 us (4%)
  matrix products  23 us (3%)
  between operations  14 us (2%)
    reduce_scatter x1, waiting for transfers between devices, local(): lax.psum_scatter(bins_out.astype(jnp.bfloat16), 'dp', scatter_dimension=1...  222 us
    reduce_scatter x1, waiting for transfers between devices, local(): lax.psum_scatter(bins_in.astype(jnp.bfloat16), 'dp', scatter_dimension=1,...  198 us
    psum x1, waiting for transfers between devices, local(): summed = lax.psum(partial_grad.astype(jnp.bfloat16), 'tensor')  124 us
    all_gather x1, waiting for transfers between devices, local(): lax.all_gather(tokens, 'tensor', axis=1, tiled=True)  46.5 us
    all_gather x1, waiting for transfers between devices, local(): lax.all_gather(out_grad, 'tensor', axis=1, tiled=True)  40.3 us
  transfers between devices with their start and end apart: 5, of which 5 were waited for; matrix products, arithmetic and copies ran while one was open for 3% of the time, Pallas kernels for 0%

commit v1 on v0

--- a/solution.py
+++ b/solution.py
@@ -8,10 +8,23 @@
 clip_limit = 4.0
 
 
+def ring_gather(x, axis, dim):
+    ways = lax.axis_size(axis)
+    up = [(d, (d + 1) % ways) for d in range(ways)]
+    down = [(d, (d - 1) % ways) for d in range(ways)]
+    earlier, later = ([x], [x])
+    for _ in range(ways // 2):
+        earlier.append(lax.ppermute(earlier[-1], axis, up))
+    for _ in range((ways - 1) // 2):
+        later.append(lax.ppermute(later[-1], axis, down))
+    line = jnp.concatenate([*earlier[::-1], *later[1:]], axis=dim)
+    return jnp.roll(line, (lax.axis_index(axis) - ways // 2) * x.shape[dim], axis=dim)
+
+
 def local(tokens, out_grad, w_in, w_out, block_rows, block_cols):
     bin_scale = 4194304.0 / lax.axis_size("dp")
     whole_tokens, whole_grad = (
-        lax.all_gather(tokens, "tensor", axis=1, tiled=True),
+        ring_gather(tokens, "tensor", 1),
         lax.all_gather(out_grad, "tensor", axis=1, tiled=True),
     )
     tok_count = whole_tokens.shape[0]

time: 699 us -> 676 us (0.967)
  waiting for transfers between devices: 631 us -> 574 us
  starting transfers between devices: 0.39 us -> 35.6 us
    all_gather x1 -> x0, waiting for transfers between devices: 46.5 us -> none  [local(): lax.all_gather(tokens, 'tensor', axis=1, tiled=True)]
    ppermute x0 -> x15, starting transfers between devices: none -> 35.2 us  [the longest x7 32.5 us: ring_gather(): later.append(lax.ppermute(later[-1], axis, down))]
    all_gather x1, waiting for transfers between devices: 40.3 us -> 18.4 us  [local(): lax.all_gather(out_grad, 'tensor', axis=1, tiled=True)]
    ppermute x0 -> x15, waiting for transfers between devices: none -> 10.8 us  [the longest x8 8.38 us: ring_gather(): earlier.append(lax.ppermute(earlier[-1], axis, up))]
  transfers between devices with their start and end apart: 5 -> 19, of which waited for: 5 -> 15; matrix products, arithmetic and copies ran while one was open for 3% -> 5% of each run, Pallas kernels for 0% -> 0%
where the time goes in v1:
time: 676 us; the launch traced here: 675 us
  waiting for transfers between devices  574 us (85%)
  starting transfers between devices  35.6 us (5%)
  local copies, waits for them, and re-layouts  24.8 us (4%)
  matrix products  23.6 us (3%)
  between operations  14.2 us (2%)
    reduce_scatter x1, waiting for transfers between devices, local(): lax.psum_scatter(bins_out.astype(jnp.bfloat16), 'dp', scatter_dimension=1...  222 us
    reduce_scatter x1, waiting for transfers between devices, local(): lax.psum_scatter(bins_in.astype(jnp.bfloat16), 'dp', scatter_dimension=1,...  199 us
    psum x1, waiting for transfers between devices, local(): summed = lax.psum(partial_grad.astype(jnp.bfloat16), 'tensor')  124 us
    ppermute x7, starting transfers between devices, ring_gather(): later.append(lax.ppermute(later[-1], axis, down))  32.5 us
    all_gather x1, waiting for transfers between devices, local(): lax.all_gather(out_grad, 'tensor', axis=1, tiled=True)  18.4 us
  transfers between devices with their start and end apart: 19, of which 15 were waited for; matrix products, arithmetic and copies ran while one was open for 5% of the time, Pallas kernels for 0%

profile of v1, /device:TPU:1, one launch (start us, length us, event | category | flops | bytes accessed | tf_op | source)
XLA Modules:
  0.0 675.3 jit_solution(1077240285103685817)
XLA Ops:
  7.2 1.1 copy.18
  8.3 2.7 collective-permute-start
  11.0 5.0 collective-permute-done
  16.0 4.8 collective-permute-start.8
  21.8 4.6 collective-permute-start.9
  27.4 4.6 collective-permute-start.10
  33.0 4.6 collective-permute-start.11
  38.5 1.6 copy.15
  40.2 4.8 collective-permute-start.12
  45.9 4.5 collective-permute-start.13
  51.4 4.6 collective-permute-start.14
  57.5 2.9 copy.22
  60.4 2.4 gather_fusion.1
  63.4 4.5 multiply_convert_fusion
  67.9 18.4 %all-gather.2.cloned.1.call-done = bf16[256,4096]{0,1:T(8,128)(2,1)} async-done(((bf16[256,256]{0,1:T(8,128)(2,1)}), bf16[256,4096]{0,1:T(8,128)(2,1)}) %all-gather.2.cloned.1.call-update) | async-done | bytes 2097168 | tf_op jit(solution)/shard_map/all_gather | solution.py:28
  86.3 3.2 copy.16
  89.5 1.9 gather_fusion
  91.5 2.3 fusion.24
  93.8 3.7 fusion.20
  98.4 2.3 floor_convert_fusion.1
  100.8 1.4 copy.55
  102.5 2.0 gather_fusion.3
  104.5 2.8 floor_convert_fusion
  107.3 1.4 copy.54
  109.4 6.7 fusion.6
  116.1 2.3 copy.53
  118.4 198.6 %reduce-scatter.3.cloned.1.call-done = bf16[24,512]{1,0:T(8,128)(2,1)} async-done(((bf16[24,16384]{1,0:T(8,128)(2,1)}), bf16[24,512]{1,0:T(8,128)(2,1)}) %reduce-scatter.3.cloned.1.call-update) | async-done | bytes 24592 | tf_op jit(solution)/shard_map/reduce_scatter | solution.py:80
  317.0 1.4 convert_multiply_fusion.1
  318.3 221.8 %reduce-scatter.5.cloned.1.call-done = bf16[24,512]{1,0:T(8,128)(2,1)} async-done(((bf16[24,16384]{1,0:T(8,128)(2,1)}), bf16[24,512]{1,0:T(8,128)(2,1)}) %reduce-scatter.5.cloned.1.call-update) | async-done | bytes 24592 | tf_op jit(solution)/shard_map/reduce_scatter | solution.py:83
  540.2 1.4 convert_multiply_fusion
  541.5 124.1 %all-reduce.2.cloned.1.call-done = bf16[256,4096]{1,0:T(8,128)(2,1)} async-done(((bf16[256,4096]{1,0:T(8,128)(2,1)}), bf16[256,4096]{1,0:T(8,128)(2,1)}) %all-reduce.2.cloned.1.call-update) | async-done | bytes 2097168 | tf_op jit(solution)/shard_map/psum | solution.py:62
  665.6 3.1 copy.88
  (79 shorter events, 9.6 us)
Async XLA Ops:
  7.2 55.6 %copy-start = (bf16[24,128,128]{2,1,0:T(8,128)(2,1)S(1)}, bf16[24,128,128]{2,1,0:T(8,128)(2,1)}, u32[]{:S(2)}) copy-start(bf16[24,128,128]{2,1,0:T(8,128)(2,1)} %param.12) | copy-start | bytes 2359300
  7.2 79.1 %all-gather.2.cloned.1.call-start = ((), (), s32[]{:S(2)}) async-start(), calls=%async_computation.2 | async-start | bytes 2228224 | tf_op jit(solution)/shard_map/all_gather | solution.py:28
  8.3 7.7 %collective-permute-start = (bf16[256,256]{0,1:T(8,128)(2,1)S(1)}, bf16[256,256]{0,1:T(8,128)(2,1)S(1)}, u32[]{:S(2)}, u32[]{:S(2)}) collective-permute-start(bf16[256,256]{0,1:T(8,128)(2,1)S(1)} %copy.18), channel_id=1, source_target_pairs={{0,1},{1,2},{2,3},{3,4},{4,5},{5,6},{6,7},{7,8},{8,9},{9,10},{10,1... | collective-permute-start | bytes 393224 | tf_op jit(solution)/shard_map/ppermute | solution.py:17
  16.0 5.6 collective-permute-start.1
  16.0 5.7 collective-permute-start.8
  21.6 5.6 collective-permute-start.2
  21.8 5.6 collective-permute-start.9
  27.2 5.6 collective-permute-start.3
  27.4 5.6 collective-permute-start.10
  32.8 5.6 collective-permute-start.4
  33.0 7.2 %collective-permute-start.11 = (bf16[256,256]{0,1:T(8,128)(2,1)S(1)}, bf16[256,256]{0,1:T(8,128)(2,1)S(1)}, u32[]{:S(2)}, u32[]{:S(2)}) collective-permute-start(bf16[256,256]{0,1:T(8,128)(2,1)S(1)} %collective-permute-done.10), channel_id=1, source_target_pairs={{0,15},{1,0},{2,1},{3,2},{4,3},{5,4},{6,5},{7,6},{8,7},{9,8},{10,9... | collective-permute-start | bytes 393224 | tf_op jit(solution)/shard_map/ppermute | solution.py:19
  38.4 6.5 collective-permute-start.5
  40.1 276.9 %reduce-scatter.3.cloned.1.call-start = ((), (), s32[]{:S(2)}) async-start(), calls=%async_computation.4 | async-start | bytes 811008 | tf_op jit(solution)/shard_map/reduce_scatter | solution.py:80
  40.2 5.8 collective-permute-start.12
  45.0 5.5 collective-permute-start.6
  45.9 5.5 collective-permute-start.13
  50.4 5.6 collective-permute-start.7
  51.4 5.6 collective-permute-start.14
  62.8 5.1 copy-start.1
  91.5 2.3 copy-start.3
  102.2 438.0 %reduce-scatter.5.cloned.1.call-start = ((), (), s32[]{:S(2)}) async-start(), calls=%async_computation.5 | async-start | bytes 811008 | tf_op jit(solution)/shard_map/reduce_scatter | solution.py:83
  104.5 4.3 copy-start.2
  108.7 556.9 %all-reduce.2.cloned.1.call-start = ((), (), s32[]{:S(2)}) async-start(), calls=%async_computation.3 | async-start | bytes 4194304 | tf_op jit(solution)/shard_map/psum | solution.py:62
Sparse Core Ops, SparseCore 0:
  40.2 46.0 all-gather.1
  102.3 214.6 reduce-scatter.2
  321.4 218.7 reduce-scatter.4
  543.0 122.6 all-reduce.1

commit v2 on v0

--- a/solution.py
+++ b/solution.py
@@ -46,7 +46,7 @@
     hidden_picked = jnp.take(hidden, safe_cols, axis=0)
     slot_terms = jnp.einsum("sth,sdh->std", dpre_picked, w_in, preferred_element_type=jnp.float32)
     partial_grad = jnp.einsum("sr,std->rtd", row_hot, slot_terms, precision=highest)
-    summed = lax.psum(partial_grad.astype(jnp.bfloat16), "tensor")
+    summed = jnp.sum(lax.all_gather(partial_grad.astype(jnp.bfloat16), "tensor"), axis=0)
     in_grad = summed.transpose(1, 0, 2).reshape(tok_count, width)
     grad_in = (
         jnp.einsum("stk,sth->skh", picked, dpre_picked, preferred_element_type=jnp.float32)

time: 699 us -> 766 us (1.096)
  waiting for transfers between devices: 631 us -> 690 us
  other arithmetic: 3.43 us -> 15 us
    all_gather x0 -> x1, waiting for transfers between devices: none -> 181 us  [local(): lax.all_gather(partial_grad.astype(jnp.bfloat16), 'tensor')]
    psum x1 -> x0, waiting for transfers between devices: 124 us -> none  [local(): summed = lax.psum(partial_grad.astype(jnp.bfloat16), 'tensor')]
    reduce_sum x0 -> x1, other arithmetic: none -> 11.6 us  [local(): jnp.sum(lax.all_gather(partial_grad.astype(jnp.bfloat16), 'tensor'), axis=0)]
where the time goes in v2:
time: 766 us; the launch traced here: 765 us
  waiting for transfers between devices  690 us (90%)
  local copies, waits for them, and re-layouts  24.5 us (3%)
  matrix products  22 us (3%)
  other arithmetic  15 us (2%)
  between operations  14 us (2%)
    reduce_scatter x1, waiting for transfers between devices, local(): lax.psum_scatter(bins_out.astype(jnp.bfloat16), 'dp', scatter_dimension=1...  222 us
    reduce_scatter x1, waiting for transfers between devices, local(): lax.psum_scatter(bins_in.astype(jnp.bfloat16), 'dp', scatter_dimension=1,...  200 us
    all_gather x1, waiting for transfers between devices, local(): lax.all_gather(partial_grad.astype(jnp.bfloat16), 'tensor')  181 us
    all_gather x1, waiting for transfers between devices, local(): lax.all_gather(tokens, 'tensor', axis=1, tiled=True)  46.5 us
    all_gather x1, waiting for transfers between devices, local(): lax.all_gather(out_grad, 'tensor', axis=1, tiled=True)  40.3 us
  transfers between devices with their start and end apart: 5, of which 5 were waited for; matrix products, arithmetic and copies ran while one was open for 3% of the time, Pallas kernels for 0%

profile of v2, /device:TPU:1, one launch (start us, length us, event | category | flops | bytes accessed | tf_op | source)
XLA Modules:
  0.0 765.4 jit_solution(4234487696986205068)
XLA Ops:
  7.2 1.7 copy.18
  9.0 1.7 copy.15
  10.8 0.7 compare_and_fusion
  11.5 46.5 %all-gather.7.cloned.1.call-done = bf16[256,4096]{0,1:T(8,128)(2,1)} async-done(((bf16[256,256]{0,1:T(8,128)(2,1)}), bf16[256,4096]{0,1:T(8,128)(2,1)}) %all-gather.7.cloned.1.call-update) | async-done | bytes 2097168 | tf_op jit(solution)/shard_map/all_gather | solution.py:14
  58.0 3.2 copy.19
  61.2 40.3 %all-gather.5.cloned.1.call-done = bf16[256,4096]{0,1:T(8,128)(2,1)} async-done(((bf16[256,256]{0,1:T(8,128)(2,1)}), bf16[256,4096]{0,1:T(8,128)(2,1)}) %all-gather.5.cloned.1.call-update) | async-done | bytes 2097168 | tf_op jit(solution)/shard_map/all_gather | solution.py:15
  101.5 4.1 copy.16
  105.6 1.9 gather_fusion.1
  107.5 2.5 gather_fusion
  110.1 0.6 fusion.24
  110.7 0.5 copy-done.2
  111.2 0.8 copy-done.3
  112.0 0.6 fusion.25
  112.7 3.6 multiply_convert_fusion
  116.3 3.7 fusion.20
  120.0 0.1 copy.21
  120.0 0.8 gather_fusion.2
  120.9 2.3 floor_convert_fusion.1
  123.2 1.4 copy.52
  124.7 0.2 reduce-scatter.5.cloned.1.call-start
  125.0 1.9 gather_fusion.3
  126.9 2.8 floor_convert_fusion
  129.7 1.4 copy.51
  131.3 0.6 fusion.26
  131.9 7.7 fusion.6
  139.6 199.7 %reduce-scatter.3.cloned.1.call-done = bf16[24,512]{1,0:T(8,128)(2,1)} async-done(((bf16[24,16384]{1,0:T(8,128)(2,1)}), bf16[24,512]{1,0:T(8,128)(2,1)}) %reduce-scatter.3.cloned.1.call-update) | async-done | bytes 24592 | tf_op jit(solution)/shard_map/reduce_scatter | solution.py:67
  339.3 1.4 convert_multiply_fusion.1
  340.6 221.7 %reduce-scatter.5.cloned.1.call-done = bf16[24,512]{1,0:T(8,128)(2,1)} async-done(((bf16[24,16384]{1,0:T(8,128)(2,1)}), bf16[24,512]{1,0:T(8,128)(2,1)}) %reduce-scatter.5.cloned.1.call-update) | async-done | bytes 24592 | tf_op jit(solution)/shard_map/reduce_scatter | solution.py:70
  562.3 1.4 convert_multiply_fusion
  563.7 181.2 %all-gather.9.cloned.1.call-done = bf16[512,256,128]{2,0,1:T(8,128)(2,1)} async-done(((bf16[32,256,128]{2,0,1:T(8,128)(2,1)}), bf16[512,256,128]{2,0,1:T(8,128)(2,1)}) %all-gather.9.cloned.1.call-update) | async-done | bytes 33554448 | tf_op jit(solution)/shard_map/all_gather | solution.py:49
  744.9 11.6 %reduce_sum.12 = bf16[32,256,128]{2,0,1:T(8,128)(2,1)S(1)} reduce(bf16[16,32,256,128]{3,1,0,2:T(8,128)(2,1)} %bitcast.42, bf16[]{:T(256)} %constant.27.clone.1), dimensions={0}, to_apply=%region_0.0 | reduce | flops 15728640 | bytes 35651584 | tf_op jit(solution)/shard_map/reduce_sum | solution.py:49
  756.6 2.3 copy.50
  (24 shorter events, 0.4 us)
Async XLA Ops:
  7.2 104.0 %copy-start = (bf16[24,128,128]{2,1,0:T(8,128)(2,1)S(1)}, bf16[24,128,128]{2,1,0:T(8,128)(2,1)}, u32[]{:S(2)}) copy-start(bf16[24,128,128]{2,1,0:T(8,128)(2,1)} %param.12) | copy-start | bytes 2359300
  7.2 50.8 %all-gather.7.cloned.1.call-start = ((), (), s32[]{:S(2)}) async-start(), calls=%async_computation.3 | async-start | bytes 2228224 | tf_op jit(solution)/shard_map/all_gather | solution.py:14
  9.0 92.5 %all-gather.5.cloned.1.call-start = ((), (), s32[]{:S(2)}) async-start(), calls=%async_computation.2 | async-start | bytes 2228224 | tf_op jit(solution)/shard_map/all_gather | solution.py:15
  10.7 328.6 %reduce-scatter.3.cloned.1.call-start = ((), (), s32[]{:S(2)}) async-start(), calls=%async_computation.4 | async-start | bytes 811008 | tf_op jit(solution)/shard_map/reduce_scatter | solution.py:67
  107.5 2.5 copy-start.4
  110.0 1.2 copy-start.2
  110.1 2.0 copy-start.3
  124.7 437.6 %reduce-scatter.5.cloned.1.call-start = ((), (), s32[]{:S(2)}) async-start(), calls=%async_computation.5 | async-start | bytes 811008 | tf_op jit(solution)/shard_map/reduce_scatter | solution.py:70
  129.7 1.5 copy-start.5
  131.2 613.7 %all-gather.9.cloned.1.call-start = ((), (), s32[]{:S(2)}) async-start(), calls=%async_computation.6 | async-start | bytes 35651584 | tf_op jit(solution)/shard_map/all_gather | solution.py:49
  756.5 2.3 copy-start.1
Sparse Core Ops, SparseCore 0:
  10.1 47.7 all-gather.6
  60.7 40.7 all-gather.4
  124.8 214.4 reduce-scatter.2
  343.5 218.7 reduce-scatter.4
  564.9 179.9 all-gather.8
